TPU v7x, 32 devices: a whole 2x2x4 slice. The times are simulated.
32 devices in a mesh: groups: 2 (over y), arc: 4 (over z), sec: 2 (over x), rep: 2 (over core).
Axes of the slice: x: 2, y: 2, z: 4, core: 2. Of those that a mesh axis runs over, the one named last changes fastest.
Arguments:
- slip_state: float32 [4096, 256], P(('groups', 'arc', 'sec', 'rep')), parts along dimension 0, may hold values from -6 to 6
- strain: float32 [6, 4096], P(None, ('groups', 'arc', 'sec', 'rep')), parts along dimension 1, may hold values from -6 to 6
- counts: int32 [4096], P(('groups', 'arc', 'sec', 'rep')), parts along dimension 0, may hold values from 1 to 12, as said below
- element_stiffness: float32 [6, 6, 4096], P(None, None, ('groups', 'arc', 'sec', 'rep')), parts along dimension 2, as said below
- foundation: float32 [6, 4096], P(None, ('groups', 'arc', 'sec', 'rep')), parts along dimension 1, may hold values from 0.01 to 0.1
- external_load: float32 [6, 4096], P(None, ('groups', 'arc', 'sec', 'rep')), parts along dimension 1, may hold values from -6 to 6
- stiffness_micro: float32 [256, 256], replicated, as said below
- tangent_inverse: float32 [256, 256], replicated
- friction_limit: float32 [256], replicated, may hold values from 0.2 to 2
- slip_scale: float32 [256], replicated, may hold values from 0.3 to 3
- section_map: float32 [6, 256], replicated, may hold values from -2.5 to 2.5
Outputs:
- new_slip: float32 [4096, 256], P(('groups', 'arc', 'sec', 'rep')), parts along dimension 0
- increment: float32 [6, 4096], P(None, ('groups', 'arc', 'sec', 'rep')), parts along dimension 1
There are 2 independent parts, one for each index of `groups`. A program takes and returns all parts, laid end to end along the dimension named above; an argument that names none is the same for every part. Nothing has to cross between parts.
Inputs may be any that keep to these rules, and one draw needn't show every extreme that they name: counts[p] is the number of slip sweeps of node p in each Newton iteration. Every element_stiffness[:, :, i] is symmetric and each diagonal entry exceeds the sum of the magnitudes of the other entries of its row. stiffness_micro is symmetric and each diagonal entry exceeds the sum of the magnitudes of the other entries of its row.
All inputs are finite; a program needn't handle non-finite values.
Results may differ from a plain program's by a relative error of at most 0.00055.
Values sent between devices are 32-bit elements; how exact they have to be, the bound alone decides.
A program may use at most 64 MiB of HBM per device.

v0:
```python
import functools
import math

import jax
import jax.numpy as jnp
from jax import lax
from jax.experimental import pallas as pl
from jax.experimental.pallas import tpu as pltpu
from jax.sharding import PartitionSpec as P

NEWTON = 2
MAXC = 12
SUB = 8
LANES = 128
ROPE = ("arc", "sec", "rep")
MESH = pl.DeviceIdType.MESH
highest = lax.Precision.HIGHEST


def split(values):
    high = values.astype(jnp.bfloat16)
    low = (values - high.astype(jnp.float32)).astype(jnp.bfloat16)
    return high, low


def bdot(left, right):
    return jnp.dot(left, right, preferred_element_type=jnp.float32)


def block_product(left, right):
    total = left[:, 0:1, :] * right[0:1]
    for k in range(1, left.shape[0]):
        total = total + left[:, k : k + 1, :] * right[k : k + 1]
    return total


def block_solve(matrix, parts):
    size = matrix.shape[0]
    for pivot in range(size):
        scale = 1.0 / matrix[pivot : pivot + 1, pivot : pivot + 1, :]
        factor = matrix[:, pivot : pivot + 1, :]

        def eliminated(values):
            row = values[pivot : pivot + 1] * scale
            rest = values - factor * row
            rows = [rest[:pivot]] * (pivot > 0) + [row] + [rest[pivot + 1 :]] * (pivot < size - 1)
            return jnp.concatenate(rows, 0)

        parts = [eliminated(values) for values in parts]
        if pivot < size - 1:
            matrix = eliminated(matrix)
    return parts


def doubling(state, steps, least, most):
    size, _, lanes = state[0].shape
    shape = (size, SUB, lanes)
    lane = lax.broadcasted_iota(jnp.int32, shape, 2)
    identity = jnp.where(
        lax.broadcasted_iota(jnp.int32, shape, 0) == lax.broadcasted_iota(jnp.int32, shape, 1),
        1.0,
        0.0,
    )

    def level(_, carry):
        s, lower, upper, rest = carry
        a, b, e = block_solve(lower + upper + rest, carry[1:])
        no_left = lane < least + s
        no_right = lane >= most - s

        def rolled(values, shift):
            return pltpu.roll(values.reshape(size * SUB, lanes), shift, 1).reshape(shape)

        a_left = jnp.where(no_left, identity, rolled(a, s))
        e_left = jnp.where(no_left, 0.0, rolled(e, s))
        b_right = jnp.where(no_right, identity, rolled(b, lanes - s))
        e_right = jnp.where(no_right, 0.0, rolled(e, lanes - s))
        rest = rest + block_product(lower, e_left) + block_product(upper, e_right)
        return s * 2, block_product(lower, a_left), block_product(upper, b_right), rest

    _, lower, upper, rest = lax.fori_loop(0, steps, level, (jnp.int32(1), *state))
    return block_solve(lower + upper + rest, [lower, upper, rest])


def kernel(
    sizes,
    slip_ref,
    strain_ref,
    counts_ref,
    element_ref,
    foundation_ref,
    load_ref,
    micro_ref,
    tangent_ref,
    limit_ref,
    scale_ref,
    map_ref,
    slip_out,
    increment_out,
    weights,
    sent,
    held,
    send_sem,
    recv_sem,
):
    group = lax.axis_index("groups")
    arc_count, sec_count, rep_count = sizes
    total = arc_count * sec_count * rep_count
    me = (
        lax.axis_index("arc") * sec_count + lax.axis_index("sec")
    ) * rep_count + lax.axis_index("rep")

    def place(index):
        return (
            group,
            index // (sec_count * rep_count),
            index // rep_count % sec_count,
            index % rep_count,
        )

    barrier = pltpu.get_barrier_semaphore()

    def greet(step, carry):
        pl.semaphore_signal(
            barrier, inc=1, device_id=place((me + step) % total), device_id_type=MESH
        )
        return carry

    lax.fori_loop(1, total, greet, 0)

    points, slips = slip_ref.shape
    size = strain_ref.shape[0]

    tangent = tangent_ref[...]
    product = jnp.dot(micro_ref[...], tangent, precision=highest, preferred_element_type=jnp.float32)
    product_high, product_low = split(product)
    tangent_high, tangent_low = split(tangent)
    weights[0 * slips : 1 * slips, :] = product_high
    weights[1 * slips : 2 * slips, :] = product_high
    weights[2 * slips : 3 * slips, :] = product_low
    weights[3 * slips : 4 * slips, :] = tangent_high
    weights[4 * slips : 5 * slips, :] = tangent_high
    weights[5 * slips : 6 * slips, :] = tangent_low
    section = map_ref[...]
    section_tangent = jnp.dot(
        section, tangent, precision=highest, preferred_element_type=jnp.float32
    )
    moved_loads = lax.dot_general(
        strain_ref[...],
        section_tangent,
        (((0,), (0,)), ((), ())),
        precision=highest,
        preferred_element_type=jnp.float32,
    )
    sweeps = jnp.broadcast_to(counts_ref[...], (LANES, points)).T
    sweeps = jnp.concatenate([sweeps] * (slips // LANES), 1)
    limit = jnp.broadcast_to(limit_ref[...], (SUB, slips))[:1]
    inverse_scale = 1.0 / scale_ref[...]
    slip = slip_ref[...]
    for newton in range(NEWTON):
        weighted = moved_loads * ((newton + 1.0) / NEWTON)

        def sweep(step, values):
            friction = limit * jnp.tanh(values * inverse_scale)
            value_high, value_low = split(values)
            friction_high, friction_low = split(friction)
            left = jnp.concatenate(
                [value_high, value_low, value_high, friction_high, friction_low, friction_high], 1
            )
            change = weighted - bdot(left, weights[...])
            return jnp.where(step.astype(jnp.float32) < sweeps, values + change, values)

        slip = lax.fori_loop(0, MAXC, sweep, slip)
    slip_out[...] = slip

    stress = lax.dot_general(
        section,
        slip,
        (((1,), (1,)), ((), ())),
        precision=highest,
        preferred_element_type=jnp.float32,
    ) * (1.0 / math.sqrt(slips))
    forcing = load_ref[...] - stress

    element = jnp.concatenate(
        [element_ref[...], jnp.zeros((size, SUB - size, points), jnp.float32)], 1
    )
    shape = (size, SUB, points)
    row = lax.broadcasted_iota(jnp.int32, shape, 0)
    column = lax.broadcasted_iota(jnp.int32, shape, 1)
    lane = lax.broadcasted_iota(jnp.int32, shape, 2)

    def rolled(values, shift):
        lanes = values.shape[2]
        return pltpu.roll(values.reshape(size * SUB, lanes), shift, 1).reshape(values.shape)

    before = jnp.where(lane == 0, 0.0, rolled(element, 1))
    foundation = jnp.concatenate(
        [foundation_ref[i : i + 1, :][None] for i in range(size)], 0
    )
    forces = jnp.concatenate([forcing[i : i + 1, :][None] for i in range(size)], 0)
    support = jnp.where(row == column, foundation, 0.0) + jnp.where(column == size, forces, 0.0)
    levels = math.ceil(math.log2(points))
    a, b, e = doubling((before, element, support), levels, 1, points)

    first = jnp.concatenate(
        [
            block_product(element, rolled(b, points - 1)),
            support + block_product(element, rolled(e, points - 1)),
        ],
        0,
    ).reshape(2 * size * SUB, points)
    last = jnp.concatenate([block_product(element, a), block_product(element, e)], 0).reshape(
        2 * size * SUB, points
    )
    fill = jnp.zeros((LANES - 2 * size * SUB, points), jnp.float32)
    first = jnp.concatenate([first, fill], 0).T[0:1]
    last = jnp.concatenate([last, fill], 0).T[points - 1 : points]
    packed = jnp.concatenate([first, last], 0)
    sent[...] = packed
    held[me] = packed
    pl.semaphore_wait(barrier, total - 1)

    def copy(step, slot, peer):
        return pltpu.make_async_remote_copy(
            src_ref=sent,
            dst_ref=held.at[slot],
            send_sem=send_sem.at[step],
            recv_sem=recv_sem.at[slot],
            device_id=place(peer),
            device_id_type=MESH,
        )

    def send(step, carry):
        copy(step, me, (me + step) % total).start()
        return carry

    lax.fori_loop(1, total, send, 0)

    def receive(step, carry):
        peer = (me + step) % total
        copy(step, peer, peer).wait_recv()
        return carry

    lax.fori_loop(1, total, receive, 0)

    wide = -(-total // LANES) * LANES

    def columns(values):
        if wide > total:
            values = jnp.concatenate([values, jnp.zeros((wide - total, LANES), jnp.float32)], 0)
        turned = [values[k : k + LANES].T for k in range(0, wide, LANES)]
        turned = turned[0] if len(turned) == 1 else jnp.concatenate(turned, 1)
        return turned[: 2 * size * SUB].reshape(2, size, SUB, wide)

    own = columns(held[:, 0, :])
    other = columns(held[:, 1, :])
    lane = lax.broadcasted_iota(jnp.int32, (size, SUB, wide), 2)
    from_left = jnp.where(lane == 0, 0.0, rolled(other[0], 1))
    support = own[1] + jnp.where(lane == 0, 0.0, rolled(other[1], 1))
    state = (from_left, own[0], support)
    faces = doubling(state, math.ceil(math.log2(total)), 0, total)[2][:, size, :]
    lane = lax.broadcasted_iota(jnp.int32, (size, wide), 1)

    def face(index):
        chosen = jnp.where((lane == index) & (lane < total), faces, 0.0)
        return jnp.sum(chosen, axis=1, keepdims=True)

    def padded(values):
        return jnp.concatenate([values, jnp.zeros((SUB - size, 1), jnp.float32)], 0)[None]

    own_face, next_face = face(me), face(me + 1)
    increment = e[:, size, :] + jnp.sum(a * padded(own_face) + b * padded(next_face), axis=1)
    lane = lax.broadcasted_iota(jnp.int32, (size, points), 1)
    increment_out[...] = jnp.where(lane == 0, own_face, increment)

    def sent_all(step, carry):
        copy(step, me, (me + step) % total).wait_send()
        return carry

    lax.fori_loop(1, total, sent_all, 0)


def solution(mesh):
    sizes = tuple(mesh.shape[axis] for axis in ROPE)
    total = math.prod(sizes)
    nodes = P(("groups",) + ROPE)
    along = P(None, ("groups",) + ROPE)

    def shards(slip, strain, counts, element, foundation, load, micro, tangent, limit, scale, section):
        slips = slip.shape[1]
        vmem = pl.BlockSpec(memory_space=pltpu.VMEM)
        return pl.pallas_call(
            functools.partial(kernel, sizes),
            out_shape=(
                jax.ShapeDtypeStruct(slip.shape, jnp.float32),
                jax.ShapeDtypeStruct(strain.shape, jnp.float32),
            ),
            in_specs=[vmem] * 11,
            out_specs=(vmem, vmem),
            scratch_shapes=[
                pltpu.VMEM((6 * slips, slips), jnp.bfloat16),
                pltpu.VMEM((2, LANES), jnp.float32),
                pltpu.VMEM((total, 2, LANES), jnp.float32),
                pltpu.SemaphoreType.DMA((total,)),
                pltpu.SemaphoreType.DMA((total,)),
            ],
            compiler_params=pltpu.CompilerParams(
                collective_id=0, has_side_effects=True, vmem_limit_bytes=32 << 20
            ),
            name="rope",
        )(
            slip,
            strain,
            counts.astype(jnp.float32).reshape(1, -1),
            element,
            foundation,
            load,
            micro,
            tangent,
            limit.reshape(1, -1),
            scale.reshape(1, -1),
            section,
        )

    return jax.shard_map(
        shards,
        mesh=mesh,
        in_specs=(
            P(("groups",) + ROPE, None),
            along,
            nodes,
            P(None, None, ("groups",) + ROPE),
            along,
            along,
            P(),
            P(),
            P(),
            P(),
            P(),
        ),
        out_specs=(P(("groups",) + ROPE, None), along),
        check_vma=False,
    )
```

profile of v0, /device:TPU:0, one launch (start us, length us, event | category | flops | bytes accessed | tf_op | source)
XLA Modules:
  0.0 27.1 jit_solution(2845482015125830067)
XLA Ops:
  0.6 0.0 copy-start.5
  0.6 0.0 copy-start.8
  0.7 0.7 %convert_bitcast_fusion.counts_ref = f32[1,128]{1,0:T(1,128)S(1)} fusion(s32[128]{0:T(128)} %param.13), kind=kLoop, calls=%fused_computation | loop fusion | flops 128 | bytes 1024 | tf_op jit(solution)/shard_map/reshape | solution.py:315
  1.3 0.0 copy-done.5
  1.3 0.0 copy-done.8
  1.3 0.0 copy-start
  1.3 0.9 %copy-done = f32[256,256]{1,0:T(8,128)S(1)} copy-done((f32[256,256]{1,0:T(8,128)S(1)}, f32[256,256]{1,0:T(8,128)}, u32[]{:S(2)}) %copy-start) | copy-done | bytes 262168
  2.3 0.0 copy-start.1
  2.3 0.9 %copy-done.1 = f32[256,256]{1,0:T(8,128)S(1)} copy-done((f32[256,256]{1,0:T(8,128)S(1)}, f32[256,256]{1,0:T(8,128)}, u32[]{:S(2)}) %copy-start.1) | copy-done | bytes 262168
  3.2 0.0 copy-start.2
  3.2 0.9 %copy-done.2 = f32[128,256]{1,0:T(8,128)S(1)} copy-done((f32[128,256]{1,0:T(8,128)S(1)}, f32[128,256]{1,0:T(8,128)}, u32[]{:S(2)}) %copy-start.2) | copy-done | bytes 131096
  4.1 0.0 copy-start.3
  4.1 0.7 %copy-done.3 = f32[6,6,128]{2,1,0:T(8,128)S(1)} copy-done((f32[6,6,128]{2,1,0:T(8,128)S(1)}, f32[6,6,128]{2,1,0:T(8,128)}, u32[]{:S(2)}) %copy-start.3) | copy-done | bytes 18456
  4.9 0.0 copy-start.4
  4.9 0.7 %copy-done.4 = f32[6,256]{1,0:T(8,128)S(1)} copy-done((f32[6,256]{1,0:T(8,128)S(1)}, f32[6,256]{1,0:T(8,128)}, u32[]{:S(2)}) %copy-start.4) | copy-done | bytes 6168
  5.6 0.0 copy-start.6
  5.6 0.7 %copy-done.6 = f32[6,128]{1,0:T(8,128)S(1)} copy-done((f32[6,128]{1,0:T(8,128)S(1)}, f32[6,128]{1,0:T(8,128)}, u32[]{:S(2)}) %copy-start.6) | copy-done | bytes 3096
  6.3 0.0 copy-start.7
  6.3 0.7 %copy-done.7 = f32[6,128]{1,0:T(8,128)S(1)} copy-done((f32[6,128]{1,0:T(8,128)S(1)}, f32[6,128]{1,0:T(8,128)}, u32[]{:S(2)}) %copy-start.7) | copy-done | bytes 3096
  6.9 0.0 copy-start.9
  6.9 0.7 %copy-done.9 = f32[256]{0:T(256)S(1)} copy-done((f32[256]{0:T(256)S(1)}, f32[256]{0:T(256)}, u32[]{:S(2)}) %copy-start.9) | copy-done | bytes 1048
  7.6 18.2 %rope.1 = (f32[128,256]{1,0:T(8,128)S(1)}, f32[6,128]{1,0:T(8,128)S(1)}) custom-call(f32[128,256]{1,0:T(8,128)S(1)} %copy-done.2, f32[6,128]{1,0:T(8,128)S(1)} %copy-done.5, f32[1,128]{1,0:T(1,128)S(1)} %convert_bitcast_fusion.counts_ref, f32[6,6,128]{2,1,0:T(8,128)S(1)} %copy-done.3, f32[6,128]{1,0:T(8,128)S(1)} %copy-done.6, f32[6,128]{1,0:T(8,128)S(1)} %copy-done.7, ...), custom_call_target="tpu_custom_call" | custom-call | tf_op jit(solution)/shard_map/rope/pallas_call | solution.py:293
  25.8 0.7 %copy.15 = f32[128,256]{1,0:T(8,128)} copy(f32[128,256]{1,0:T(8,128)S(1)} %get-tuple-element.4) | data formatting | bytes 262144
  26.5 0.6 %copy.16 = f32[6,128]{1,0:T(8,128)} copy(f32[6,128]{1,0:T(8,128)S(1)} %get-tuple-element.5) | data formatting | bytes 6144
Async XLA Ops:
  0.6 0.7 %copy-start.5 = (f32[6,128]{1,0:T(8,128)S(1)}, f32[6,128]{1,0:T(8,128)}, u32[]{:S(2)}) copy-start(f32[6,128]{1,0:T(8,128)} %strain_ref.1) | copy-start | bytes 9220
  0.6 0.7 %copy-start.8 = (f32[256]{0:T(256)S(1)}, f32[256]{0:T(256)}, u32[]{:S(2)}) copy-start(f32[256]{0:T(256)} %param.19) | copy-start | bytes 3076
  1.3 0.9 %copy-start = (f32[256,256]{1,0:T(8,128)S(1)}, f32[256,256]{1,0:T(8,128)}, u32[]{:S(2)}) copy-start(f32[256,256]{1,0:T(8,128)} %micro_ref.1) | copy-start | bytes 786436
  2.3 0.9 %copy-start.1 = (f32[256,256]{1,0:T(8,128)S(1)}, f32[256,256]{1,0:T(8,128)}, u32[]{:S(2)}) copy-start(f32[256,256]{1,0:T(8,128)} %tangent_ref.1) | copy-start | bytes 786436
  3.2 0.9 %copy-start.2 = (f32[128,256]{1,0:T(8,128)S(1)}, f32[128,256]{1,0:T(8,128)}, u32[]{:S(2)}) copy-start(f32[128,256]{1,0:T(8,128)} %slip_ref.1) | copy-start | bytes 393220
  4.1 0.7 %copy-start.3 = (f32[6,6,128]{2,1,0:T(8,128)S(1)}, f32[6,6,128]{2,1,0:T(8,128)}, u32[]{:S(2)}) copy-start(f32[6,6,128]{2,1,0:T(8,128)} %element_ref.1) | copy-start | bytes 55300
  4.9 0.7 %copy-start.4 = (f32[6,256]{1,0:T(8,128)S(1)}, f32[6,256]{1,0:T(8,128)}, u32[]{:S(2)}) copy-start(f32[6,256]{1,0:T(8,128)} %map_ref.1) | copy-start | bytes 18436
  5.6 0.7 %copy-start.6 = (f32[6,128]{1,0:T(8,128)S(1)}, f32[6,128]{1,0:T(8,128)}, u32[]{:S(2)}) copy-start(f32[6,128]{1,0:T(8,128)} %foundation_ref.1) | copy-start | bytes 9220
  6.3 0.7 %copy-start.7 = (f32[6,128]{1,0:T(8,128)S(1)}, f32[6,128]{1,0:T(8,128)}, u32[]{:S(2)}) copy-start(f32[6,128]{1,0:T(8,128)} %load_ref.1) | copy-start | bytes 9220
  6.9 0.7 %copy-start.9 = (f32[256]{0:T(256)S(1)}, f32[256]{0:T(256)}, u32[]{:S(2)}) copy-start(f32[256]{0:T(256)} %param.20) | copy-start | bytes 3076
where the time goes:
time: 27.5 us; the launch traced here: 27.1 us
  Pallas kernels  18.2 us (66%)
  local copies, waits for them, and re-layouts  7.55 us (27%)
  other arithmetic  0.67 us (2%)
  between operations  0.67 us (2%)
    pallas_call x1, Pallas kernels, shards(): pl.pallas_call(functools.partial(kernel, sizes), out_shape=(jax.ShapeDtyp...  18.2 us
    unnamed x22, local copies, waits for them, and re-layouts  7.55 us
    reshape x1, other arithmetic, shards(): counts.astype(jnp.float32).reshape(1, -1)  0.67 us

commit v1 on v0

--- a/solution.py
+++ b/solution.py
@@ -10,6 +10,8 @@
 
 NEWTON = 2
 MAXC = 12
+OPERANDS = 11
+ORDER = (7, 6, 10, 1, 0, 2, 8, 9, 3, 4, 5)
 SUB = 8
 LANES = 128
 ROPE = ("arc", "sec", "rep")
@@ -82,27 +84,28 @@
     return block_solve(lower + upper + rest, [lower, upper, rest])
 
 
-def kernel(
-    sizes,
-    slip_ref,
-    strain_ref,
-    counts_ref,
-    element_ref,
-    foundation_ref,
-    load_ref,
-    micro_ref,
-    tangent_ref,
-    limit_ref,
-    scale_ref,
-    map_ref,
-    slip_out,
-    increment_out,
-    weights,
-    sent,
-    held,
-    send_sem,
-    recv_sem,
-):
+def kernel(sizes, *refs):
+    given, (slip_out, increment_out), rest = refs[:OPERANDS], refs[OPERANDS : OPERANDS + 2], refs[OPERANDS + 2 :]
+    local, (weights, held, load_sem, send_sem, recv_sem) = rest[:OPERANDS], rest[OPERANDS:]
+    copies = [
+        pltpu.make_async_copy(source, target, load_sem.at[k])
+        for k, (source, target) in enumerate(zip(given, local))
+    ]
+    for k in ORDER:
+        copies[k].start()
+    (
+        slip_ref,
+        strain_ref,
+        counts_ref,
+        element_ref,
+        foundation_ref,
+        load_ref,
+        micro_ref,
+        tangent_ref,
+        limit_ref,
+        scale_ref,
+        map_ref,
+    ) = local
     group = lax.axis_index("groups")
     arc_count, sec_count, rep_count = sizes
     total = arc_count * sec_count * rep_count
@@ -120,16 +123,26 @@
 
     barrier = pltpu.get_barrier_semaphore()
 
-    def greet(step, carry):
-        pl.semaphore_signal(
-            barrier, inc=1, device_id=place((me + step) % total), device_id_type=MESH
+    def peer(step):
+        return (me + step) % total
+
+    def each(act):
+        if total <= 16:
+            for step in range(1, total):
+                act(step)
+        else:
+            pl.loop(1, total)(act)
+
+    each(
+        lambda step: pl.semaphore_signal(
+            barrier, inc=1, device_id=place(peer(step)), device_id_type=MESH
         )
-        return carry
-
-    lax.fori_loop(1, total, greet, 0)
+    )
 
     points, slips = slip_ref.shape
     size = strain_ref.shape[0]
+    for k in ORDER:
+        copies[k].wait()
 
     tangent = tangent_ref[...]
     product = jnp.dot(micro_ref[...], tangent, precision=highest, preferred_element_type=jnp.float32)
@@ -152,7 +165,7 @@
         precision=highest,
         preferred_element_type=jnp.float32,
     )
-    sweeps = jnp.broadcast_to(counts_ref[...], (LANES, points)).T
+    sweeps = jnp.broadcast_to(counts_ref[...].astype(jnp.float32), (LANES, points)).T
     sweeps = jnp.concatenate([sweeps] * (slips // LANES), 1)
     limit = jnp.broadcast_to(limit_ref[...], (SUB, slips))[:1]
     inverse_scale = 1.0 / scale_ref[...]
@@ -217,32 +230,21 @@
     first = jnp.concatenate([first, fill], 0).T[0:1]
     last = jnp.concatenate([last, fill], 0).T[points - 1 : points]
     packed = jnp.concatenate([first, last], 0)
-    sent[...] = packed
     held[me] = packed
     pl.semaphore_wait(barrier, total - 1)
 
-    def copy(step, slot, peer):
+    def copy(step, slot):
         return pltpu.make_async_remote_copy(
-            src_ref=sent,
+            src_ref=held.at[slot],
             dst_ref=held.at[slot],
             send_sem=send_sem.at[step],
             recv_sem=recv_sem.at[slot],
-            device_id=place(peer),
+            device_id=place(peer(step)),
             device_id_type=MESH,
         )
 
-    def send(step, carry):
-        copy(step, me, (me + step) % total).start()
-        return carry
-
-    lax.fori_loop(1, total, send, 0)
-
-    def receive(step, carry):
-        peer = (me + step) % total
-        copy(step, peer, peer).wait_recv()
-        return carry
-
-    lax.fori_loop(1, total, receive, 0)
+    each(lambda step: copy(step, me).start())
+    each(lambda step: copy(step, peer(step)).wait_recv())
 
     wide = -(-total // LANES) * LANES
 
@@ -274,11 +276,7 @@
     lane = lax.broadcasted_iota(jnp.int32, (size, points), 1)
     increment_out[...] = jnp.where(lane == 0, own_face, increment)
 
-    def sent_all(step, carry):
-        copy(step, me, (me + step) % total).wait_send()
-        return carry
-
-    lax.fori_loop(1, total, sent_all, 0)
+    each(lambda step: copy(step, me).wait_send())
 
 
 def solution(mesh):
@@ -289,30 +287,10 @@
 
     def shards(slip, strain, counts, element, foundation, load, micro, tangent, limit, scale, section):
         slips = slip.shape[1]
-        vmem = pl.BlockSpec(memory_space=pltpu.VMEM)
-        return pl.pallas_call(
-            functools.partial(kernel, sizes),
-            out_shape=(
-                jax.ShapeDtypeStruct(slip.shape, jnp.float32),
-                jax.ShapeDtypeStruct(strain.shape, jnp.float32),
-            ),
-            in_specs=[vmem] * 11,
-            out_specs=(vmem, vmem),
-            scratch_shapes=[
-                pltpu.VMEM((6 * slips, slips), jnp.bfloat16),
-                pltpu.VMEM((2, LANES), jnp.float32),
-                pltpu.VMEM((total, 2, LANES), jnp.float32),
-                pltpu.SemaphoreType.DMA((total,)),
-                pltpu.SemaphoreType.DMA((total,)),
-            ],
-            compiler_params=pltpu.CompilerParams(
-                collective_id=0, has_side_effects=True, vmem_limit_bytes=32 << 20
-            ),
-            name="rope",
-        )(
+        operands = (
             slip,
             strain,
-            counts.astype(jnp.float32).reshape(1, -1),
+            counts.reshape(1, -1),
             element,
             foundation,
             load,
@@ -322,6 +300,28 @@
             scale.reshape(1, -1),
             section,
         )
+        vmem = pl.BlockSpec(memory_space=pltpu.VMEM)
+        return pl.pallas_call(
+            functools.partial(kernel, sizes),
+            out_shape=(
+                jax.ShapeDtypeStruct(slip.shape, jnp.float32),
+                jax.ShapeDtypeStruct(strain.shape, jnp.float32),
+            ),
+            in_specs=[pl.BlockSpec(memory_space=pltpu.HBM)] * OPERANDS,
+            out_specs=(vmem, vmem),
+            scratch_shapes=[pltpu.VMEM(value.shape, value.dtype) for value in operands]
+            + [
+                pltpu.VMEM((6 * slips, slips), jnp.bfloat16),
+                pltpu.VMEM((total, 2, LANES), jnp.float32),
+                pltpu.SemaphoreType.DMA((OPERANDS,)),
+                pltpu.SemaphoreType.DMA((total,)),
+                pltpu.SemaphoreType.DMA((total,)),
+            ],
+            compiler_params=pltpu.CompilerParams(
+                collective_id=0, has_side_effects=True, vmem_limit_bytes=32 << 20
+            ),
+            name="rope",
+        )(*[pltpu.with_memory_space_constraint(value, pltpu.HBM) for value in operands])
 
     return jax.shard_map(
         shards,

time: 27.5 us -> 21.3 us (0.77); the launches traced: 27.1 us -> 21.2 us
  local copies, waits for them, and re-layouts: 7.55 us -> 1.25 us
  Pallas kernels: 18.2 us -> 19.3 us
  other arithmetic: 0.67 us -> 0 us
    unnamed x22 -> x2, local copies, waits for them, and re-layouts: 7.55 us -> 1.25 us
    pallas_call x1, Pallas kernels: 18.2 us -> 19.3 us  [shards(): pl.pallas_call(functools.partial(kernel, sizes), out_shape=(jax.ShapeDtyp...]
    reshape x1 -> x0, other arithmetic: 0.67 us -> none  [shards(): counts.astype(jnp.float32).reshape(1, -1)]
where the time goes in v1:
time: 21.3 us; the launch traced here: 21.2 us
  Pallas kernels  19.3 us (91%)
  local copies, waits for them, and re-layouts  1.25 us (6%)
  between operations  0.64 us (3%)
    pallas_call x1, Pallas kernels, shards(): pl.pallas_call(functools.partial(kernel, sizes), out_shape=(jax.ShapeDtyp...  19.3 us
    unnamed x2, local copies, waits for them, and re-layouts  1.25 us

profile of v1, /device:TPU:0, one launch (start us, length us, event | category | flops | bytes accessed | tf_op | source)
XLA Modules:
  0.0 21.2 jit_solution(15555703713030366687)
XLA Ops:
  0.6 19.3 %rope.1 = (f32[128,256]{1,0:T(8,128)S(1)}, f32[6,128]{1,0:T(8,128)S(1)}) custom-call(f32[128,256]{1,0:T(8,128)} %refs_0_.1, f32[6,128]{1,0:T(8,128)} %refs_1_.1, s32[1,128]{1,0:T(1,128)} %bitcast.5, f32[6,6,128]{2,1,0:T(8,128)} %refs_3_.1, f32[6,128]{1,0:T(8,128)} %refs_4_.1, f32[6,128]{1,0:T(8,128)} %refs_5_.1, f32[256,256]{1,0:T(8,128)} %refs_6_.1, ...), custom_call_target="tpu_custom_call" | custom-call | tf_op jit(solution)/shard_map/rope/pallas_call | solution.py:304
  19.9 0.7 %copy.15 = f32[128,256]{1,0:T(8,128)} copy(f32[128,256]{1,0:T(8,128)S(1)} %get-tuple-element.4) | data formatting | bytes 262144
  20.6 0.6 %copy.16 = f32[6,128]{1,0:T(8,128)} copy(f32[6,128]{1,0:T(8,128)S(1)} %get-tuple-element.5) | data formatting | bytes 6144

commit v2 on v1

--- a/solution.py
+++ b/solution.py
@@ -54,7 +54,7 @@
     return parts
 
 
-def doubling(state, steps, least, most):
+def doubling(state, steps, least, most, beside=None, others=()):
     size, _, lanes = state[0].shape
     shape = (size, SUB, lanes)
     lane = lax.broadcasted_iota(jnp.int32, shape, 2)
@@ -64,9 +64,11 @@
         0.0,
     )
 
-    def level(_, carry):
-        s, lower, upper, rest = carry
-        a, b, e = block_solve(lower + upper + rest, carry[1:])
+    def level(step, carry):
+        s, lower, upper, rest, *others = carry
+        a, b, e = block_solve(lower + upper + rest, [lower, upper, rest])
+        if beside is not None:
+            others = [beside(step, *others)]
         no_left = lane < least + s
         no_right = lane >= most - s
 
@@ -78,10 +80,12 @@
         b_right = jnp.where(no_right, identity, rolled(b, lanes - s))
         e_right = jnp.where(no_right, 0.0, rolled(e, lanes - s))
         rest = rest + block_product(lower, e_left) + block_product(upper, e_right)
-        return s * 2, block_product(lower, a_left), block_product(upper, b_right), rest
-
-    _, lower, upper, rest = lax.fori_loop(0, steps, level, (jnp.int32(1), *state))
-    return block_solve(lower + upper + rest, [lower, upper, rest])
+        return s * 2, block_product(lower, a_left), block_product(upper, b_right), rest, *others
+
+    _, lower, upper, rest, *others = lax.fori_loop(
+        0, steps, level, (jnp.int32(1), *state, *others)
+    )
+    return (*block_solve(lower + upper + rest, [lower, upper, rest]), *others)
 
 
 def kernel(sizes, *refs):
@@ -170,6 +174,25 @@
     limit = jnp.broadcast_to(limit_ref[...], (SUB, slips))[:1]
     inverse_scale = 1.0 / scale_ref[...]
     slip = slip_ref[...]
+    element = jnp.concatenate(
+        [element_ref[...], jnp.zeros((size, SUB - size, points), jnp.float32)], 1
+    )
+    shape = (size, SUB, points)
+    row = lax.broadcasted_iota(jnp.int32, shape, 0)
+    column = lax.broadcasted_iota(jnp.int32, shape, 1)
+    lane = lax.broadcasted_iota(jnp.int32, shape, 2)
+
+    def rolled(values, shift):
+        lanes = values.shape[2]
+        return pltpu.roll(values.reshape(size * SUB, lanes), shift, 1).reshape(values.shape)
+
+    before = jnp.where(lane == 0, 0.0, rolled(element, 1))
+    foundation = jnp.concatenate(
+        [foundation_ref[i : i + 1, :][None] for i in range(size)], 0
+    )
+    support = jnp.where(row == column, foundation, 0.0)
+    levels = math.ceil(math.log2(points))
+
     for newton in range(NEWTON):
         weighted = moved_loads * ((newton + 1.0) / NEWTON)
 
@@ -183,7 +206,15 @@
             change = weighted - bdot(left, weights[...])
             return jnp.where(step.astype(jnp.float32) < sweeps, values + change, values)
 
-        slip = lax.fori_loop(0, MAXC, sweep, slip)
+        done = 0
+        if newton == 0 and levels <= MAXC:
+            done = levels
+            a, b, e, slip = doubling(
+                (before, element, support), levels, 1, points, sweep, (slip,)
+            )
+        elif newton == 0:
+            a, b, e = doubling((before, element, support), levels, 1, points)
+        slip = lax.fori_loop(done, MAXC, sweep, slip)
     slip_out[...] = slip
 
     stress = lax.dot_general(
@@ -195,37 +226,36 @@
     ) * (1.0 / math.sqrt(slips))
     forcing = load_ref[...] - stress
 
-    element = jnp.concatenate(
-        [element_ref[...], jnp.zeros((size, SUB - size, points), jnp.float32)], 1
-    )
-    shape = (size, SUB, points)
-    row = lax.broadcasted_iota(jnp.int32, shape, 0)
-    column = lax.broadcasted_iota(jnp.int32, shape, 1)
-    lane = lax.broadcasted_iota(jnp.int32, shape, 2)
-
-    def rolled(values, shift):
-        lanes = values.shape[2]
-        return pltpu.roll(values.reshape(size * SUB, lanes), shift, 1).reshape(values.shape)
-
-    before = jnp.where(lane == 0, 0.0, rolled(element, 1))
-    foundation = jnp.concatenate(
-        [foundation_ref[i : i + 1, :][None] for i in range(size)], 0
-    )
     forces = jnp.concatenate([forcing[i : i + 1, :][None] for i in range(size)], 0)
-    support = jnp.where(row == column, foundation, 0.0) + jnp.where(column == size, forces, 0.0)
-    levels = math.ceil(math.log2(points))
-    a, b, e = doubling((before, element, support), levels, 1, points)
-
+    support_loaded = support + jnp.where(column == size, forces, 0.0)
+
+    def condensed(blocks):
+        total_force = jnp.sum(
+            jnp.sum(jnp.where(lane == 0, 0.0, blocks) * forces, axis=0), axis=1, keepdims=True
+        )
+        spread = jnp.broadcast_to(total_force, (SUB, points))
+        return jnp.concatenate([spread[k : k + 1][None] for k in range(size)], 0)
+
+    first_force = forces + condensed(a)
+    last_force = condensed(b)
     first = jnp.concatenate(
         [
             block_product(element, rolled(b, points - 1)),
-            support + block_product(element, rolled(e, points - 1)),
+            jnp.where(
+                column == size,
+                first_force,
+                support + block_product(element, rolled(e, points - 1)),
+            ),
         ],
         0,
     ).reshape(2 * size * SUB, points)
-    last = jnp.concatenate([block_product(element, a), block_product(element, e)], 0).reshape(
-        2 * size * SUB, points
-    )
+    last = jnp.concatenate(
+        [
+            block_product(element, a),
+            jnp.where(column == size, last_force, block_product(element, e)),
+        ],
+        0,
+    ).reshape(2 * size * SUB, points)
     fill = jnp.zeros((LANES - 2 * size * SUB, points), jnp.float32)
     first = jnp.concatenate([first, fill], 0).T[0:1]
     last = jnp.concatenate([last, fill], 0).T[points - 1 : points]
@@ -244,6 +274,7 @@
         )
 
     each(lambda step: copy(step, me).start())
+    e = doubling((before, element, support_loaded), levels, 1, points)[2]
     each(lambda step: copy(step, peer(step)).wait_recv())
 
     wide = -(-total // LANES) * LANES

time: 21.3 us -> 20.1 us (0.944)
  Pallas kernels: 19.3 us -> 18.1 us
    pallas_call x1, Pallas kernels: 19.3 us -> 18.1 us  [shards(): pl.pallas_call(functools.partial(kernel, sizes), out_shape=(jax.ShapeDtyp...]
where the time goes in v2:
time: 20.1 us; the launch traced here: 20 us
  Pallas kernels  18.1 us (90%)
  local copies, waits for them, and re-layouts  1.25 us (6%)
  between operations  0.64 us (3%)
    pallas_call x1, Pallas kernels, shards(): pl.pallas_call(functools.partial(kernel, sizes), out_shape=(jax.ShapeDtyp...  18.1 us
    unnamed x2, local copies, waits for them, and re-layouts  1.25 us

profile of v2, /device:TPU:0, one launch (start us, length us, event | category | flops | bytes accessed | tf_op | source)
XLA Modules:
  0.0 20.0 jit_solution(4603228664481303614)
XLA Ops:
  0.6 18.1 %rope.1 = (f32[128,256]{1,0:T(8,128)S(1)}, f32[6,128]{1,0:T(8,128)S(1)}) custom-call(f32[128,256]{1,0:T(8,128)} %refs_0_.1, f32[6,128]{1,0:T(8,128)} %refs_1_.1, s32[1,128]{1,0:T(1,128)} %bitcast.5, f32[6,6,128]{2,1,0:T(8,128)} %refs_3_.1, f32[6,128]{1,0:T(8,128)} %refs_4_.1, f32[6,128]{1,0:T(8,128)} %refs_5_.1, f32[256,256]{1,0:T(8,128)} %refs_6_.1, ...), custom_call_target="tpu_custom_call" | custom-call | tf_op jit(solution)/shard_map/rope/pallas_call | solution.py:335
  18.7 0.7 %copy.15 = f32[128,256]{1,0:T(8,128)} copy(f32[128,256]{1,0:T(8,128)S(1)} %get-tuple-element.4) | data formatting | bytes 262144
  19.4 0.6 %copy.16 = f32[6,128]{1,0:T(8,128)} copy(f32[6,128]{1,0:T(8,128)S(1)} %get-tuple-element.5) | data formatting | bytes 6144

commit v3 on v2

--- a/solution.py
+++ b/solution.py
@@ -117,18 +117,18 @@
         lax.axis_index("arc") * sec_count + lax.axis_index("sec")
     ) * rep_count + lax.axis_index("rep")
 
-    def place(index):
+    barrier = pltpu.get_barrier_semaphore()
+
+    def partner(step):
         return (
-            group,
-            index // (sec_count * rep_count),
-            index // rep_count % sec_count,
-            index % rep_count,
-        )
-
-    barrier = pltpu.get_barrier_semaphore()
+            lax.rem(lax.axis_index("arc") + step // (sec_count * rep_count), arc_count),
+            lax.rem(lax.axis_index("sec") + step // rep_count % sec_count, sec_count),
+            lax.rem(lax.axis_index("rep") + step % rep_count, rep_count),
+        )
 
     def peer(step):
-        return (me + step) % total
+        arc, sec, rep = partner(step)
+        return (arc * sec_count + sec) * rep_count + rep
 
     def each(act):
         if total <= 16:
@@ -139,7 +139,7 @@
 
     each(
         lambda step: pl.semaphore_signal(
-            barrier, inc=1, device_id=place(peer(step)), device_id_type=MESH
+            barrier, inc=1, device_id=(group, *partner(step)), device_id_type=MESH
         )
     )
 
@@ -269,7 +269,7 @@
             dst_ref=held.at[slot],
             send_sem=send_sem.at[step],
             recv_sem=recv_sem.at[slot],
-            device_id=place(peer(step)),
+            device_id=(group, *partner(step)),
             device_id_type=MESH,
         )
 

time: 20.1 us -> 20.2 us (level)
  no operation moved by 1% of the time
where the time goes in v3:
time: 20.2 us; the launch traced here: 20 us
  Pallas kernels  18.1 us (90%)
  local copies, waits for them, and re-layouts  1.25 us (6%)
  between operations  0.64 us (3%)
    pallas_call x1, Pallas kernels, shards(): pl.pallas_call(functools.partial(kernel, sizes), out_shape=(jax.ShapeDtyp...  18.1 us
    unnamed x2, local copies, waits for them, and re-layouts  1.25 us

profile of v3, /device:TPU:0, one launch (start us, length us, event | category | flops | bytes accessed | tf_op | source)
XLA Modules:
  0.0 20.0 jit_solution(9554762662304272462)
XLA Ops:
  0.6 18.1 %rope.1 = (f32[128,256]{1,0:T(8,128)S(1)}, f32[6,128]{1,0:T(8,128)S(1)}) custom-call(f32[128,256]{1,0:T(8,128)} %refs_0_.1, f32[6,128]{1,0:T(8,128)} %refs_1_.1, s32[1,128]{1,0:T(1,128)} %bitcast.5, f32[6,6,128]{2,1,0:T(8,128)} %refs_3_.1, f32[6,128]{1,0:T(8,128)} %refs_4_.1, f32[6,128]{1,0:T(8,128)} %refs_5_.1, f32[256,256]{1,0:T(8,128)} %refs_6_.1, ...), custom_call_target="tpu_custom_call" | custom-call | tf_op jit(solution)/shard_map/rope/pallas_call | solution.py:335
  18.8 0.7 %copy.15 = f32[128,256]{1,0:T(8,128)} copy(f32[128,256]{1,0:T(8,128)S(1)} %get-tuple-element.4) | data formatting | bytes 262144
  19.4 0.6 %copy.16 = f32[6,128]{1,0:T(8,128)} copy(f32[6,128]{1,0:T(8,128)S(1)} %get-tuple-element.5) | data formatting | bytes 6144
